TPU v7x, 128 devices: a whole 4x4x4 slice. The times are simulated.
128 devices in a mesh: row: 8 (over y, core), col: 16 (over x, z).
Axes of the slice: x: 4, y: 4, z: 4, core: 2. Of those that a mesh axis runs over, the one named last changes fastest.
Arguments:
- descriptors: bfloat16 [16384, 1024], P(('row', 'col'))
- gradients: bfloat16 [3, 4, 16384, 1024], P(None, None, ('row', 'col'))
- sparse_panel: bfloat16 [512, 1024], P('col')
- sparse_trail: bfloat16 [2048, 1024], P('col')
- atom_counts: int32 [128, 8], P(('row', 'col')), may hold values from 1 to 16, 64 in all within a row
- owner_rows: int32 [128, 8], P(('row', 'col')), may hold values from 0 to 7, each once within a row
- neighbor_ids: int32 [1024, 16, 4], P(('row', 'col')), may hold values from 0 to 65519
Outputs:
- panel_factor: float32 [512, 512], replicated
- cross_factor: float32 [2048, 512], P('col')
- trail_residual: float32 [2048, 65536], P('col', 'row')
Inputs may be any that keep to these rules, and one draw needn't show every extreme that they name: `atom_counts`: the structures of one device's line hold 64 atoms together, and every line has a structure of 16 atoms. `owner_rows`: every device gives exactly one structure to each row group.
All inputs are finite; a program needn't handle non-finite values.
Results may differ from a plain program's by a relative error of at most 0.0043.
Values may be sent and summed in bfloat16 or wider, within the bound.
No kernel may reach another device: no remote copies, remote signals or barrier semaphores. Data moves between devices by JAX's collectives and lax.ppermute only.
A program may use at most 128 MiB of HBM per device.

v0:
```python
import jax
import jax.numpy as jnp
from jax import lax
from jax.sharding import PartitionSpec as P

ridge_value = 0.1


def slot_rows(environments, desc_here, slope_here, count_here, neighbor_here, owner_here):
    struct_count = count_here.shape[0]
    atom_slots = neighbor_here.shape[1]
    neighbor_count = neighbor_here.shape[2]
    env_count = environments.shape[0]
    correlation = lax.dot_general(
        environments, desc_here, (((1,), (1,)), ((), ())), preferred_element_type=jnp.float32
    )
    slope_dots = lax.dot_general(
        environments, slope_here, (((1,), (1,)), ((), ())), preferred_element_type=jnp.float32
    )
    slope_dots = slope_dots.reshape(env_count, 3, neighbor_count, struct_count, atom_slots)
    slot_index = jnp.arange(atom_slots, dtype=jnp.int32)
    live_mask = (slot_index[None, :] < count_here[:, None]).astype(jnp.float32)
    squares = (correlation * correlation).reshape(env_count, struct_count, atom_slots)
    energy = jnp.sum(squares * live_mask[None], axis=2) / count_here.astype(jnp.float32)[None, :]
    partner = neighbor_here % count_here[:, None, None]
    struct_index = jnp.arange(struct_count, dtype=jnp.int32)
    flat_index = (struct_index[:, None, None] * atom_slots + partner).reshape(-1)
    picked = jnp.take(correlation, flat_index, axis=1).reshape(
        env_count, struct_count, atom_slots, neighbor_count
    )
    picked = jnp.transpose(picked, (0, 3, 1, 2))
    forces = -2.0 * jnp.sum(picked[:, None] * slope_dots, axis=2) * live_mask[None, None]
    forces = jnp.transpose(forces, (0, 2, 3, 1)).reshape(env_count, struct_count, 3 * atom_slots)
    padding = jnp.zeros((env_count, struct_count, atom_slots - 1), jnp.float32)
    slot_values = jnp.concatenate([energy[:, :, None], forces, padding], axis=2).astype(
        jnp.bfloat16
    )
    chosen = (owner_here[None, :] == struct_index[:, None]).astype(jnp.int32)
    owner_order = jnp.sum(struct_index[None, :] * chosen, axis=1)
    return jnp.take(slot_values, owner_order, axis=1)


def factor_panel(gram_sum, cross_sum, total_rows):
    gram_matrix = gram_sum / total_rows + ridge_value * jnp.eye(
        gram_sum.shape[0], dtype=jnp.float32
    )
    lower_factor = jnp.linalg.cholesky(gram_matrix)
    coupling = lax.linalg.triangular_solve(
        lower_factor, cross_sum / total_rows, left_side=True, lower=True
    )
    weights = lax.linalg.triangular_solve(
        lower_factor, coupling, left_side=True, lower=True, transpose_a=True
    )
    return (lower_factor.T, coupling, weights)


def split_weights(weights):
    weight_high = weights.astype(jnp.bfloat16)
    held_high = lax.optimization_barrier(weight_high)
    weight_low = (weights - held_high.astype(jnp.float32)).astype(jnp.bfloat16)
    return (weight_high, weight_low)


def reduce_products(gram_part, cross_part):
    return lax.psum((gram_part, cross_part), ("row", "col"))


def contract_rows(left_side, right_side):
    return lax.dot_general(
        left_side, right_side, (((1,), (1,)), ((), ())), preferred_element_type=jnp.float32
    )


def contract_cols(left_side, right_side):
    return lax.dot_general(
        left_side, right_side, (((0,), (0,)), ((), ())), preferred_element_type=jnp.float32
    )


def arrange_direct(block_rows, row_count, col_count):
    env_width = block_rows.shape[0] // col_count
    slot_count = block_rows.shape[2]
    shaped = block_rows.reshape(col_count, env_width, row_count, slot_count)
    return jnp.transpose(shaped, (2, 0, 1, 3)).reshape(row_count * col_count, env_width, slot_count)


def restore_direct(block_rows, row_count, col_count):
    env_width = block_rows.shape[1]
    slot_count = block_rows.shape[2]
    shaped = block_rows.reshape(row_count, col_count, env_width, slot_count)
    return jnp.transpose(shaped, (2, 1, 0, 3)).reshape(
        env_width, row_count * col_count * slot_count
    )


def per_device(
    descriptors, gradients, sparse_panel, sparse_trail, atom_counts, owner_rows, neighbor_ids
):
    row_count = lax.axis_size("row")
    col_count = lax.axis_size("col")
    col_index = lax.axis_index("col")
    count_here = atom_counts[0]
    owner_here = owner_rows[0]
    slope_here = gradients.reshape(-1, gradients.shape[3])
    panel_width = sparse_panel.shape[0]
    trail_width = sparse_trail.shape[0]
    panel_total = panel_width * col_count
    trail_total = trail_width * col_count
    slot_count = 4 * neighbor_ids.shape[1]
    total_rows = row_count * row_count * col_count * slot_count
    own_envs = jnp.concatenate([sparse_panel, sparse_trail], axis=0)
    kernel_rows = slot_rows(
        lax.all_gather(own_envs, "col", axis=0, tiled=True),
        descriptors,
        slope_here,
        count_here,
        neighbor_ids,
        owner_here,
    )
    blocks = kernel_rows.reshape(col_count, panel_width + trail_width, row_count, slot_count)
    panel_rows = blocks[:, :panel_width].reshape(panel_total, row_count, slot_count)
    trail_rows = blocks[:, panel_width:].reshape(trail_total, row_count, slot_count)
    received = (
        lax.all_to_all(
            arrange_direct(panel_rows, row_count, col_count),
            ("row", "col"),
            split_axis=0,
            concat_axis=0,
            tiled=True,
        ),
        lax.all_to_all(
            arrange_direct(trail_rows, row_count, col_count),
            ("row", "col"),
            split_axis=0,
            concat_axis=0,
            tiled=True,
        ),
    )
    panel_own = restore_direct(received[0], row_count, col_count)
    trail_own = restore_direct(received[1], row_count, col_count)
    segment = lax.all_gather(panel_own, "col", axis=0, tiled=True)
    columns = jnp.concatenate(
        [contract_rows(segment, panel_own), contract_rows(segment, trail_own)], axis=1
    )
    gram_part = lax.dynamic_update_slice(
        jnp.zeros((panel_total, panel_total), jnp.float32),
        columns[:, :panel_width],
        (0, col_index * panel_width),
    )
    cross_part = lax.dynamic_update_slice(
        jnp.zeros((panel_total, trail_total), jnp.float32),
        columns[:, panel_width:],
        (0, col_index * trail_width),
    )
    gram_sum, cross_sum = reduce_products(gram_part, cross_part)
    panel_factor, coupling, weights = factor_panel(gram_sum, cross_sum, total_rows)
    coupling_own = lax.dynamic_slice_in_dim(coupling, col_index * trail_width, trail_width, 1)
    weights_own = lax.dynamic_slice_in_dim(weights, col_index * trail_width, trail_width, 1)
    weight_high, weight_low = split_weights(weights_own)
    segment = lax.all_gather(panel_own, "col", axis=0, tiled=True)
    trail_residual = (
        trail_own.astype(jnp.float32)
        - contract_cols(weight_high, segment)
        - contract_cols(weight_low, segment)
    )
    cross_factor = coupling_own.T
    return (panel_factor, cross_factor, trail_residual)


def solution(mesh):
    return jax.shard_map(
        per_device,
        mesh=mesh,
        in_specs=(
            P(("row", "col"), None),
            P(None, None, ("row", "col"), None),
            P("col", None),
            P("col", None),
            P(("row", "col"), None),
            P(("row", "col"), None),
            P(("row", "col"), None, None),
        ),
        out_specs=(P(), P("col", None), P("col", "row")),
        check_vma=False,
    )
```

profile of v0, /device:TPU:1, one launch (start us, length us, event | category | flops | bytes accessed | tf_op | source)
XLA Modules:
  0.0 593.3 jit_solution(4389010923176962485)
XLA Ops:
  14.9 55.6 %all-gather.3.cloned.1.call-done = bf16[2560,1024]{1,0:T(8,128)(2,1)} async-done(((bf16[160,1024]{1,0:T(8,128)(2,1)}), bf16[2560,1024]{1,0:T(8,128)(2,1)}) %all-gather.3.cloned.1.call-update) | async-done | bytes 5242896 | tf_op jit(solution)/shard_map/all_gather | solution.py:113
  70.5 5.5 multiply_reduce_fusion.1
  75.9 7.7 %gather_fusion = f32[512,2560]{1,0:T(8,128)} fusion(f32[2560,128]{0,1:T(8,128)} %get-tuple-element.64, s32[1024]{0:T(1024)S(1)} %pad_clamp_fusion.1), kind=kCustom, calls=%fused_computation | custom fusion | bytes 10487808 | tf_op jit(solution)/shard_map/jit(_take)/gather | solution.py:28
  83.6 7.1 %gather.17 = f32[2560,8,16,4]{0,3,2,1:T(4,128)} reshape(f32[2560,512]{0,1:T(8,128)} %bitcast.121) | data formatting | bytes 10485760 | tf_op jit(solution)/shard_map/jit(_take)/gather | solution.py:28
  90.7 4.6 fusion.1
  95.4 12.1 %multiply_reduce_fusion = f32[2560,3,8,16]{0,3,2,1:T(8,128)S(1)} fusion(f32[2560,4,8,16]{0,3,2,1:T(8,128)S(1)} %fusion.1, bf16[3,4,8,16,1024]{4,3,2,1,0:T(8,128)(2,1)S(1)} %bitcast.117, bf16[2560,1024]{1,0:T(8,128)(2,1)} %all-gather.3.cloned.1.call-done), kind=kOutput, calls=%fused_computation.4 | convolution fusion | flops 8059944960 | bytes 17563648 | tf_op jit(solution)/shard_map/dot_general | solution.py:17
  112.8 8.5 %gather.19 = bf16[16,160,8,64]{1,0,3,2:T(8,128)(2,1)} reshape(bf16[2560,8,64]{0,2,1:T(8,128)(2,1)} %bitcast.120) | data formatting | bytes 5242880 | tf_op jit(solution)/shard_map/jit(_take)/gather | solution.py:40
  128.9 21.1 %all_to_all.10 = bf16[128,2,1024]{2,1,0:T(2,128)(2,1)S(1)} all-to-all(bf16[128,2,1024]{2,1,0:T(2,128)(2,1)S(1)} %reshape.290), channel_id=1, replica_groups=mesh['row'=8,'col'=16] {'row','col'}, dimensions={0} | all-to-all | bytes 1048576 | tf_op jit(solution)/shard_map/all_to_all | solution.py:124
  152.9 4.3 slice.149
  157.3 4.8 all-to-all-start.1
  162.2 36.1 %all-to-all-done.1 = bf16[128,128,64]{1,2,0:T(8,128)(2,1)S(1)} async-done(((bf16[128,128,64]{1,2,0:T(8,128)(2,1)}), bf16[128,128,64]{1,2,0:T(8,128)(2,1)S(1)}, u32[]{:S(2)}, u32[]{:S(2)}) %all-to-all-start.1) | async-done | bytes 2097184 | tf_op jit(solution)/shard_map/all_to_all | solution.py:131
  199.9 40.1 %all-gather.5.cloned.1.call-done = bf16[512,8192]{1,0:T(8,128)(2,1)} async-done(((bf16[32,8192]{1,0:T(8,128)(2,1)}), bf16[512,8192]{1,0:T(8,128)(2,1)}) %all-gather.5.cloned.1.call-update) | async-done | bytes 8388624 | tf_op jit(solution)/shard_map/all_gather | solution.py:141
  240.1 6.1 %convolution_dynamic-update-slice_fusion.3 = f32[512,512]{0,1:T(8,128)S(1)} fusion(f32[512,512]{0,1:T(8,128)S(1)} %broadcast_in_dim.40, s32[]{:T(128)S(6)} %select_n.80, bf16[512,8192]{1,0:T(8,128)(2,1)} %all-gather.5.cloned.1.call-done, bf16[32,8192]{1,0:T(8,128)(2,1)S(1)} %copy-done.8), kind=kOutput, calls=%fused_computation.54 | convolution fusion | flops 268435456 | bytes 8978436 | tf_op jit(solution)/shard_map/dot_general | solution.py:69
  256.2 152.8 %all-reduce.4.cloned.1.call-done = (f32[512,512]{0,1:T(8,128)}, f32[512,2048]{1,0:T(8,128)}) async-done(((f32[512,512]{0,1:T(8,128)}, f32[512,2048]{1,0:T(8,128)}), (f32[512,512]{0,1:T(8,128)}, f32[512,2048]{1,0:T(8,128)})) %all-reduce.4.cloned.1.call-update) | async-done | bytes 5242896 | tf_op jit(solution)/shard_map/psum | solution.py:65
  411.1 11.7 %cholesky.103 = f32[128,128]{1,0:T(8,128)S(1)} custom-call(f32[128,128]{1,0:T(8,128)S(1)} %cholesky.263), custom_call_target="Cholesky" | custom-call | tf_op jit(solution)/shard_map/jit(cholesky)/cholesky | solution.py:47
  423.0 9.8 %custom-call.32 = f32[1,128,128]{1,2,0:T(8,128)S(1)} custom-call(f32[1,128,128]{2,1,0:T(8,128)S(1)} %get-tuple-element.62), custom_call_target="InvertDiagBlocksLowerTriangular" | custom-call | tf_op jit(solution)/shard_map/jit(cholesky)/cholesky | solution.py:47
  433.6 11.7 %cholesky.215 = f32[128,128]{1,0:T(8,128)S(1)} custom-call(f32[128,128]{1,0:T(8,128)S(1)} %cholesky.267), custom_call_target="Cholesky" | custom-call | tf_op jit(solution)/shard_map/jit(cholesky)/cholesky | solution.py:47
  445.6 10.0 %custom-call.33 = f32[1,128,128]{1,2,0:T(8,128)S(1)} custom-call(f32[1,128,128]{2,1,0:T(8,128)S(1)} %get-tuple-element.60), custom_call_target="InvertDiagBlocksLowerTriangular" | custom-call | tf_op jit(solution)/shard_map/jit(cholesky)/cholesky | solution.py:47
  456.5 11.7 %cholesky.236 = f32[128,128]{1,0:T(8,128)S(1)} custom-call(f32[128,128]{1,0:T(8,128)S(1)} %cholesky.272), custom_call_target="Cholesky" | custom-call | tf_op jit(solution)/shard_map/jit(cholesky)/cholesky | solution.py:47
  468.4 9.8 %custom-call.34 = f32[1,128,128]{1,2,0:T(8,128)S(1)} custom-call(f32[1,128,128]{2,1,0:T(8,128)S(1)} %get-tuple-element.58), custom_call_target="InvertDiagBlocksLowerTriangular" | custom-call | tf_op jit(solution)/shard_map/jit(cholesky)/cholesky | solution.py:47
  479.0 11.9 %cholesky.253 = f32[128,128]{1,0:T(8,128)S(1)} custom-call(f32[128,128]{1,0:T(8,128)S(1)} %convolution_subtract_fusion.8), custom_call_target="Cholesky" | custom-call | tf_op jit(solution)/shard_map/jit(cholesky)/cholesky | solution.py:47
  493.7 4.8 broadcast_multiply_fusion
  502.3 11.1 %while.1 = (s32[]{:T(128)}, f32[512,512]{0,1:T(8,128)S(1)}, s32[4,2]{0,1:T(2,128)S(1)}, f32[4,128,128]{2,1,0:T(8,128)}, s32[]{:T(128)}) while((s32[]{:T(128)}, f32[512,512]{0,1:T(8,128)S(1)}, s32[4,2]{0,1:T(2,128)S(1)}, f32[4,128,128]{2,1,0:T(8,128)}, s32[]{:T(128)}) %tuple.40), condition=%wide.while_cond, body=%wide.while_body.sunk | while | flops 2 | bytes 393329 | solution.py:48
  513.5 40.2 %custom-call.35 = f32[4,128,128]{1,2,0:T(8,128)S(1)} custom-call(f32[4,128,128]{2,1,0:T(8,128)} %get-tuple-element.10), custom_call_target="InvertDiagBlocksLowerTriangular" | custom-call | tf_op jit(solution)/shard_map/triangular_solve | solution.py:48
  (143 shorter events, 87.8 us)
Async XLA Ops:
  7.2 88.2 %copy-start = (bf16[3,4,128,1024]{3,2,1,0:T(8,128)(2,1)S(1)}, bf16[3,4,128,1024]{3,2,1,0:T(8,128)(2,1)}, u32[]{:S(2)}) copy-start(bf16[3,4,128,1024]{3,2,1,0:T(8,128)(2,1)} %param.8) | copy-start | bytes 9437188
  7.2 63.3 %all-gather.3.cloned.1.call-start = ((), (), s32[]{:S(2)}) async-start(), calls=%async_computation.2 | async-start | bytes 5570560 | tf_op jit(solution)/shard_map/all_gather | solution.py:113
  9.1 230.9 %all-gather.5.cloned.1.call-start = ((), (), s32[]{:S(2)}) async-start(), calls=%async_computation.3 | async-start | bytes 8912896 | tf_op jit(solution)/shard_map/all_gather | solution.py:141
  124.9 2.0 copy-start.5
  157.3 82.8 %copy-start.8 = (bf16[32,8192]{1,0:T(8,128)(2,1)S(1)}, bf16[32,8192]{1,0:T(8,128)(2,1)}, u32[]{:S(2)}) copy-start(bf16[32,8192]{1,0:T(8,128)(2,1)} %reshape.250) | copy-start | bytes 1572868
  157.3 41.0 %all-to-all-start.1 = ((bf16[128,128,64]{1,2,0:T(8,128)(2,1)}), bf16[128,128,64]{1,2,0:T(8,128)(2,1)S(1)}, u32[]{:S(2)}, u32[]{:S(2)}) async-start(bf16[128,128,64]{1,2,0:T(8,128)(2,1)} %bitcast.123), calls=%async_computation.1 | async-start | bytes 4194304 | tf_op jit(solution)/shard_map/all_to_all | solution.py:131
  162.1 246.9 %all-reduce.4.cloned.1.call-start = ((), (), s32[]{:S(2)}) async-start(), calls=%async_computation.4 | async-start | bytes 10485760 | tf_op jit(solution)/shard_map/psum | solution.py:65
  240.1 9.7 %copy-start.2 = (bf16[512,8192]{1,0:T(8,128)(2,1)S(1)}, bf16[512,8192]{1,0:T(8,128)(2,1)}, u32[]{:S(2)}) copy-start(bf16[512,8192]{1,0:T(8,128)(2,1)} %all-gather.5.cloned.1.call-done) | copy-start | bytes 25165828
  246.2 1.0 copy-start.11
  247.2 2.5 copy-start.7
  409.0 1.8 copy-start.10
  513.5 45.9 %copy-start.9 = (f32[512,512]{0,1:T(8,128)}, f32[512,512]{0,1:T(8,128)S(1)}, u32[]{:S(2)}) copy-start(f32[512,512]{0,1:T(8,128)S(1)} %get-tuple-element.126) | copy-start | bytes 3145732
  553.7 5.8 copy-start.4
  561.8 4.3 copy-start.3
  572.9 7.8 %slice-start = ((s8[8388608]{0:T(1024)(128)(4,1)}), s8[4194304]{0:T(1024)(128)(4,1)S(1)}, s32[]{:S(2)}) async-start(s8[8388608]{0:T(1024)(128)(4,1)} %bitcast.118), calls=%async_computation.5 | async-start | bytes 8388608
  576.5 4.2 slice-start.1
  579.6 1.6 copy-start.6
  582.7 3.6 copy-start.1
Sparse Core Ops, SparseCore 0:
  10.8 59.6 all-gather.2
  153.0 86.8 all-gather.4
  253.0 156.0 all-reduce.3
where the time goes:
time: 604 us; the launch traced here: 593 us
  waiting for transfers between devices  285 us (47%)
  other arithmetic  145 us (24%)
  local copies, waits for them, and re-layouts  61.7 us (10%)
  matrix products  58.4 us (10%)
  blocking collectives  21.1 us (3%)
  between operations  17.4 us (3%)
    psum x1, waiting for transfers between devices, reduce_products(): return lax.psum((gram_part, cross_part), ('row', 'col'))  153 us
    another operation x15, other arithmetic, factor_panel(): lower_factor = jnp.linalg.cholesky(gram_matrix)  79.5 us
    all_gather x1, waiting for transfers between devices, per_device(): lax.all_gather(own_envs, 'col', axis=0, tiled=True)  55.6 us
    another operation x3, other arithmetic, factor_panel(): lax.linalg.triangular_solve(lower_factor, cross_sum / total_rows, left_si...  41.4 us
    all_gather x1, waiting for transfers between devices, per_device(): segment = lax.all_gather(panel_own, 'col', axis=0, tiled=True)  40.1 us
    all_to_all x1, waiting for transfers between devices, per_device(): lax.all_to_all(arrange_direct(trail_rows, row_count, col_count), ('row',...  36.1 us
    all_to_all x1, blocking collectives, per_device(): lax.all_to_all(arrange_direct(panel_rows, row_count, col_count), ('row',...  21.1 us
    gather x2, local copies, waits for them, and re-layouts, slot_rows(): jnp.take(correlation, flat_index, axis=1)  14.8 us
  transfers between devices with their start and end apart: 4, of which 4 were waited for; matrix products, arithmetic and copies ran while one was open for 3% of the time, Pallas kernels for 0%

commit v1 on v0

--- a/solution.py
+++ b/solution.py
@@ -4,6 +4,13 @@
 from jax.sharding import PartitionSpec as P
 
 ridge_value = 0.1
+
+
+def replace_digits_now(chip_axis, load):
+    return jnp.concatenate(
+        jax.lax.all_to_all(jnp.stack(jax.lax.axis_size(chip_axis) * [load]), chip_axis, 0, 0),
+        axis=0,
+    )
 
 
 def slot_rows(environments, desc_here, slope_here, count_here, neighbor_here, owner_here):
@@ -110,7 +117,7 @@
     total_rows = row_count * row_count * col_count * slot_count
     own_envs = jnp.concatenate([sparse_panel, sparse_trail], axis=0)
     kernel_rows = slot_rows(
-        lax.all_gather(own_envs, "col", axis=0, tiled=True),
+        replace_digits_now("col", own_envs),
         descriptors,
         slope_here,
         count_here,

time: 604 us -> 634 us (1.050); the launches traced: 593 us -> 630 us
  waiting for transfers between devices: 285 us -> 305 us
  blocking collectives: 21.1 us -> 30.1 us
  starting transfers between devices: 4.96 us -> 13.5 us
    all_to_all x0 -> x1, waiting for transfers between devices: none -> 76.3 us  [replace_digits_now(): jax.lax.all_to_all(jnp.stack(jax.lax.axis_size(chip_axis) * [load]), chip...]
    all_gather x1 -> x0, waiting for transfers between devices: 55.6 us -> none  [per_device(): lax.all_gather(own_envs, 'col', axis=0, tiled=True)]
    all_to_all x1, blocking collectives: 21.1 us -> 30.1 us  [per_device(): lax.all_to_all(arrange_direct(panel_rows, row_count, col_count), ('row',...]
    all_to_all x0 -> x1, starting transfers between devices: none -> 8.62 us  [replace_digits_now(): jax.lax.all_to_all(jnp.stack(jax.lax.axis_size(chip_axis) * [load]), chip...]
    another operation x20 -> x21, local copies, waits for them, and re-layouts: 11.1 us -> 14.1 us
  transfers between devices with their start and end apart: 4 -> 4, of which waited for: 4 -> 4; matrix products, arithmetic and copies ran while one was open for 3% -> 2% of each run, Pallas kernels for 0% -> 0%
where the time goes in v1:
time: 634 us; the launch traced here: 630 us
  waiting for transfers between devices  305 us (48%)
  other arithmetic  140 us (22%)
  local copies, waits for them, and re-layouts  64.9 us (10%)
  matrix products  58.4 us (9%)
  blocking collectives  30.1 us (5%)
  between operations  17.6 us (3%)
  starting transfers between devices  13.5 us (2%)
    psum x1, waiting for transfers between devices, reduce_products(): return lax.psum((gram_part, cross_part), ('row', 'col'))  153 us
    another operation x15, other arithmetic, factor_panel(): lower_factor = jnp.linalg.cholesky(gram_matrix)  79.7 us
    all_to_all x1, waiting for transfers between devices, replace_digits_now(): jax.lax.all_to_all(jnp.stack(jax.lax.axis_size(chip_axis) * [load]), chip...  76.3 us
    another operation x3, other arithmetic, factor_panel(): lax.linalg.triangular_solve(lower_factor, cross_sum / total_rows, left_si...  41.4 us
    all_gather x1, waiting for transfers between devices, per_device(): segment = lax.all_gather(panel_own, 'col', axis=0, tiled=True)  40.1 us
    all_to_all x1, waiting for transfers between devices, per_device(): lax.all_to_all(arrange_direct(trail_rows, row_count, col_count), ('row',...  36.1 us
    all_to_all x1, blocking collectives, per_device(): lax.all_to_all(arrange_direct(panel_rows, row_count, col_count), ('row',...  30.1 us
    gather x2, local copies, waits for them, and re-layouts, slot_rows(): jnp.take(correlation, flat_index, axis=1)  15 us
  transfers between devices with their start and end apart: 4, of which 4 were waited for; matrix products, arithmetic and copies ran while one was open for 2% of the time, Pallas kernels for 0%

profile of v1, /device:TPU:1, one launch (start us, length us, event | category | flops | bytes accessed | tf_op | source)
XLA Modules:
  0.0 629.7 jit_solution(16844791477071226365)
XLA Ops:
  11.3 8.6 %all-to-all-start = ((bf16[16,160,1024]{2,1,0:T(8,128)(2,1)}), bf16[16,160,1024]{2,1,0:T(8,128)(2,1)}, u32[]{:S(2)}, u32[]{:S(2)}) async-start(bf16[16,160,1024]{2,1,0:T(8,128)(2,1)} %stack.2), calls=%async_computation | async-start | bytes 10485760 | tf_op jit(solution)/shard_map/all_to_all | solution.py:11
  21.1 76.3 %all-to-all-done = bf16[16,160,1024]{2,1,0:T(8,128)(2,1)} async-done(((bf16[16,160,1024]{2,1,0:T(8,128)(2,1)}), bf16[16,160,1024]{2,1,0:T(8,128)(2,1)}, u32[]{:S(2)}, u32[]{:S(2)}) %all-to-all-start) | async-done | bytes 5242912 | tf_op jit(solution)/shard_map/all_to_all | solution.py:11
  97.4 5.4 multiply_reduce_fusion.1
  102.8 7.8 %gather_fusion = f32[512,2560]{1,0:T(8,128)} fusion(f32[2560,128]{0,1:T(8,128)} %get-tuple-element.64, s32[1024]{0:T(1024)S(1)} %pad_clamp_fusion.1), kind=kCustom, calls=%fused_computation | custom fusion | bytes 10487808 | tf_op jit(solution)/shard_map/jit(_take)/gather | solution.py:35
  110.7 7.1 %gather.17 = f32[2560,8,16,4]{0,3,2,1:T(4,128)} reshape(f32[2560,512]{0,1:T(8,128)} %bitcast.122) | data formatting | bytes 10485760 | tf_op jit(solution)/shard_map/jit(_take)/gather | solution.py:35
  117.8 4.6 fusion
  122.4 12.1 %multiply_reduce_fusion = f32[2560,3,8,16]{0,3,2,1:T(8,128)S(1)} fusion(f32[2560,4,8,16]{0,3,2,1:T(8,128)S(1)} %fusion, bf16[2560,1024,1,1,1]{1,0,4,3,2:T(8,128)(2,1)} %bitcast.9, bf16[3,4,8,16,1024]{4,3,2,1,0:T(8,128)(2,1)S(1)} %bitcast.118), kind=kOutput, calls=%fused_computation.4 | convolution fusion | flops 8059944960 | bytes 17563648 | tf_op jit(solution)/shard_map/dot_general | solution.py:24
  139.9 8.7 %gather.19 = bf16[16,160,8,64]{1,0,3,2:T(8,128)(2,1)} reshape(bf16[2560,8,64]{0,2,1:T(8,128)(2,1)} %bitcast.121) | data formatting | bytes 5242880 | tf_op jit(solution)/shard_map/jit(_take)/gather | solution.py:47
  156.2 30.1 %all_to_all.15 = bf16[128,2,1024]{2,1,0:T(2,128)(2,1)S(1)} all-to-all(bf16[128,2,1024]{2,1,0:T(2,128)(2,1)S(1)} %reshape.296), channel_id=1, replica_groups=mesh['row'=8,'col'=16] {'row','col'}, dimensions={0} | all-to-all | bytes 1048576 | tf_op jit(solution)/shard_map/all_to_all | solution.py:131
  193.6 4.8 all-to-all-start.2
  198.5 36.1 %all-to-all-done.2 = bf16[128,128,64]{1,2,0:T(8,128)(2,1)S(1)} async-done(((bf16[128,128,64]{1,2,0:T(8,128)(2,1)}), bf16[128,128,64]{1,2,0:T(8,128)(2,1)S(1)}, u32[]{:S(2)}, u32[]{:S(2)}) %all-to-all-start.2) | async-done | bytes 2097184 | tf_op jit(solution)/shard_map/all_to_all | solution.py:138
  236.3 40.1 %all-gather.2.cloned.1.call-done = bf16[512,8192]{1,0:T(8,128)(2,1)} async-done(((bf16[32,8192]{1,0:T(8,128)(2,1)}), bf16[512,8192]{1,0:T(8,128)(2,1)}) %all-gather.2.cloned.1.call-update) | async-done | bytes 8388624 | tf_op jit(solution)/shard_map/all_gather | solution.py:148
  276.5 6.1 convolution_dynamic-update-slice_fusion.3
  292.3 152.9 %all-reduce.4.cloned.1.call-done = (f32[512,512]{0,1:T(8,128)}, f32[512,2048]{1,0:T(8,128)}) async-done(((f32[512,512]{0,1:T(8,128)}, f32[512,2048]{1,0:T(8,128)}), (f32[512,512]{0,1:T(8,128)}, f32[512,2048]{1,0:T(8,128)})) %all-reduce.4.cloned.1.call-update) | async-done | bytes 5242896 | tf_op jit(solution)/shard_map/psum | solution.py:72
  447.2 11.7 %cholesky.103 = f32[128,128]{1,0:T(8,128)S(1)} custom-call(f32[128,128]{1,0:T(8,128)S(1)} %cholesky.263), custom_call_target="Cholesky" | custom-call | tf_op jit(solution)/shard_map/jit(cholesky)/cholesky | solution.py:54
  459.1 9.8 %custom-call.32 = f32[1,128,128]{1,2,0:T(8,128)S(1)} custom-call(f32[1,128,128]{2,1,0:T(8,128)S(1)} %get-tuple-element.62), custom_call_target="InvertDiagBlocksLowerTriangular" | custom-call | tf_op jit(solution)/shard_map/jit(cholesky)/cholesky | solution.py:54
  469.7 11.7 %cholesky.215 = f32[128,128]{1,0:T(8,128)S(1)} custom-call(f32[128,128]{1,0:T(8,128)S(1)} %cholesky.267), custom_call_target="Cholesky" | custom-call | tf_op jit(solution)/shard_map/jit(cholesky)/cholesky | solution.py:54
  481.7 10.2 %custom-call.33 = f32[1,128,128]{1,2,0:T(8,128)S(1)} custom-call(f32[1,128,128]{2,1,0:T(8,128)S(1)} %get-tuple-element.60), custom_call_target="InvertDiagBlocksLowerTriangular" | custom-call | tf_op jit(solution)/shard_map/jit(cholesky)/cholesky | solution.py:54
  492.9 11.7 %cholesky.236 = f32[128,128]{1,0:T(8,128)S(1)} custom-call(f32[128,128]{1,0:T(8,128)S(1)} %cholesky.272), custom_call_target="Cholesky" | custom-call | tf_op jit(solution)/shard_map/jit(cholesky)/cholesky | solution.py:54
  504.7 9.8 %custom-call.34 = f32[1,128,128]{1,2,0:T(8,128)S(1)} custom-call(f32[1,128,128]{2,1,0:T(8,128)S(1)} %get-tuple-element.58), custom_call_target="InvertDiagBlocksLowerTriangular" | custom-call | tf_op jit(solution)/shard_map/jit(cholesky)/cholesky | solution.py:54
  515.3 11.9 %cholesky.253 = f32[128,128]{1,0:T(8,128)S(1)} custom-call(f32[128,128]{1,0:T(8,128)S(1)} %convolution_subtract_fusion.8), custom_call_target="Cholesky" | custom-call | tf_op jit(solution)/shard_map/jit(cholesky)/cholesky | solution.py:54
  530.1 4.8 broadcast_multiply_fusion
  538.7 11.2 %while.1 = (s32[]{:T(128)}, f32[512,512]{0,1:T(8,128)S(1)}, s32[4,2]{0,1:T(2,128)S(1)}, f32[4,128,128]{2,1,0:T(8,128)}, s32[]{:T(128)}) while((s32[]{:T(128)}, f32[512,512]{0,1:T(8,128)S(1)}, s32[4,2]{0,1:T(2,128)S(1)}, f32[4,128,128]{2,1,0:T(8,128)}, s32[]{:T(128)}) %tuple.40), condition=%wide.while_cond, body=%wide.while_body.sunk | while | flops 2 | bytes 393329 | solution.py:55
  549.9 40.2 %custom-call.35 = f32[4,128,128]{1,2,0:T(8,128)S(1)} custom-call(f32[4,128,128]{2,1,0:T(8,128)} %get-tuple-element.10), custom_call_target="InvertDiagBlocksLowerTriangular" | custom-call | tf_op jit(solution)/shard_map/triangular_solve | solution.py:55
  (151 shorter events, 89.5 us)
Async XLA Ops:
  7.2 115.2 %copy-start = (bf16[3,4,128,1024]{3,2,1,0:T(8,128)(2,1)S(1)}, bf16[3,4,128,1024]{3,2,1,0:T(8,128)(2,1)}, u32[]{:S(2)}) copy-start(bf16[3,4,128,1024]{3,2,1,0:T(8,128)(2,1)} %param.8) | copy-start | bytes 9437188
  11.3 8.7 %copy-start.15 = (s32[1,8]{1,0:T(1,128)S(1)}, s32[1,8]{1,0:T(1,128)}, u32[]{:S(2)}) copy-start(s32[1,8]{1,0:T(1,128)} %param.12) | copy-start | bytes 100
  11.3 8.8 %copy-start.14 = (s32[1,8]{1,0:T(1,128)S(1)}, s32[1,8]{1,0:T(1,128)}, u32[]{:S(2)}) copy-start(s32[1,8]{1,0:T(1,128)} %param.11) | copy-start | bytes 100
  11.3 8.8 %copy-start.13 = (s32[8,16,4]{1,2,0:T(4,128)S(1)}, s32[8,16,4]{1,2,0:T(4,128)}, u32[]{:S(2)}) copy-start(s32[8,16,4]{1,2,0:T(4,128)} %param.13) | copy-start | bytes 6148
  11.3 86.1 %copy-start.12 = (bf16[128,1024]{1,0:T(8,128)(2,1)S(1)}, bf16[128,1024]{1,0:T(8,128)(2,1)}, u32[]{:S(2)}) copy-start(bf16[128,1024]{1,0:T(8,128)(2,1)} %param.7) | copy-start | bytes 786436
  11.3 86.1 %all-to-all-start = ((bf16[16,160,1024]{2,1,0:T(8,128)(2,1)}), bf16[16,160,1024]{2,1,0:T(8,128)(2,1)}, u32[]{:S(2)}, u32[]{:S(2)}) async-start(bf16[16,160,1024]{2,1,0:T(8,128)(2,1)} %stack.2), calls=%async_computation | async-start | bytes 10485760 | tf_op jit(solution)/shard_map/all_to_all | solution.py:11
  19.9 256.4 %all-gather.2.cloned.1.call-start = ((), (), s32[]{:S(2)}) async-start(), calls=%async_computation.3 | async-start | bytes 8912896 | tf_op jit(solution)/shard_map/all_gather | solution.py:148
  152.2 2.0 copy-start.5
  193.6 82.8 %copy-start.8 = (bf16[32,8192]{1,0:T(8,128)(2,1)S(1)}, bf16[32,8192]{1,0:T(8,128)(2,1)}, u32[]{:S(2)}) copy-start(bf16[32,8192]{1,0:T(8,128)(2,1)} %reshape.256) | copy-start | bytes 1572868
  193.6 41.0 %all-to-all-start.2 = ((bf16[128,128,64]{1,2,0:T(8,128)(2,1)}), bf16[128,128,64]{1,2,0:T(8,128)(2,1)S(1)}, u32[]{:S(2)}, u32[]{:S(2)}) async-start(bf16[128,128,64]{1,2,0:T(8,128)(2,1)} %bitcast.124), calls=%async_computation.2 | async-start | bytes 4194304 | tf_op jit(solution)/shard_map/all_to_all | solution.py:138
  198.5 246.7 %all-reduce.4.cloned.1.call-start = ((), (), s32[]{:S(2)}) async-start(), calls=%async_computation.4 | async-start | bytes 10485760 | tf_op jit(solution)/shard_map/psum | solution.py:72
  276.5 9.7 %copy-start.2 = (bf16[512,8192]{1,0:T(8,128)(2,1)S(1)}, bf16[512,8192]{1,0:T(8,128)(2,1)}, u32[]{:S(2)}) copy-start(bf16[512,8192]{1,0:T(8,128)(2,1)} %all-gather.2.cloned.1.call-done) | copy-start | bytes 25165828
  282.6 1.0 copy-start.11
  283.6 2.5 copy-start.7
  445.2 1.8 copy-start.10
  549.9 46.0 %copy-start.9 = (f32[512,512]{0,1:T(8,128)}, f32[512,512]{0,1:T(8,128)S(1)}, u32[]{:S(2)}) copy-start(f32[512,512]{0,1:T(8,128)S(1)} %get-tuple-element.126) | copy-start | bytes 3145732
  590.1 5.8 copy-start.4
  598.2 4.3 copy-start.3
  609.3 7.8 %slice-start = ((s8[8388608]{0:T(1024)(128)(4,1)}), s8[4194304]{0:T(1024)(128)(4,1)S(1)}, s32[]{:S(2)}) async-start(s8[8388608]{0:T(1024)(128)(4,1)} %bitcast.119), calls=%async_computation.5 | async-start | bytes 8388608
  612.9 4.2 slice-start.1
  616.0 1.6 copy-start.6
  619.1 3.6 copy-start.1
Sparse Core Ops, SparseCore 0:
  189.4 86.8 all-gather.1
  289.3 155.8 all-reduce.3
